TPU v7x, 256 devices: a whole 4x4x8 slice. The times are simulated.
256 devices in a mesh: ctx: 32 (over z, x_hi, core), tp: 8 (over y, x_lo).
Axes of the slice: x: 4 (x_hi: 2, x_lo: 2; x = x_hi * 2 + x_lo), y: 4, z: 8, core: 2. Of those that a mesh axis runs over, the one named last changes fastest.
Arguments:
- compressed: bfloat16 [4096, 1536], P('ctx', 'tp'), may hold values from -6 to 6
- latent: bfloat16 [4096, 576], P('ctx'), may hold values from -276 to 276
- w_uq: bfloat16 [1536, 12288], P(None, 'tp'), may hold values from -0.15625 to 0.15625
- w_uk: bfloat16 [512, 8192], P('ctx', 'tp'), may hold values from -0.5 to 0.5
- w_uv: bfloat16 [512, 8192], P('ctx', 'tp'), may hold values from -0.8984375 to 0.8984375
- span_ids: int32 [64], replicated, may hold values from 0 to 63, as said below
Outputs:
- attended: bfloat16 [4096, 8192], P('ctx', 'tp')
Inputs may be any that keep to these rules, and one draw needn't show every extreme that they name: `span_ids`: entries 2 d and 2 d + 1 hold spans c and 63 - c for some c < 32, in that order; every span appears once.
All inputs are finite; a program needn't handle non-finite values.
Results may differ from a plain program's by a relative error of at most 0.0085.
The roundings to bfloat16 on the way count: a program that leaves them out, or rounds other values in their place, can miss the bound.
Values may be sent and summed in bfloat16 or wider, within the bound.
No kernel may reach another device: no remote copies, remote signals or barrier semaphores. Data moves between devices by JAX's collectives and lax.ppermute only.
A program may use at most 64 MiB of HBM per device.

v0:
```python
import jax
import jax.numpy as jnp
from jax import lax
from jax.sharding import PartitionSpec as P

NOPE = 128
ROPE = 64
VDIM = 128
KV = 512


def per_device(compressed, latent, w_uq, w_uk, w_uv, span_ids):
    row_count = compressed.shape[0]
    span_len = row_count // 2
    heads_dev = w_uk.shape[1] // NOPE
    span_count = span_ids.shape[0]
    total_slots = span_count * span_len
    softmax_scale = (NOPE + ROPE) ** (-0.5)
    query_proj = jnp.dot(
        lax.all_gather(compressed, "tp", axis=1, tiled=True),
        w_uq,
        preferred_element_type=jnp.float32,
    )
    query_proj = query_proj.astype(jnp.bfloat16).reshape(row_count, heads_dev, NOPE + ROPE)
    q_nope = query_proj[:, :, :NOPE]
    q_rope = query_proj[:, :, NOPE:]
    shard_rows = lax.all_gather(w_uk, "ctx", axis=0, tiled=True)
    key_block = shard_rows.reshape(shard_rows.shape[0], heads_dev, NOPE)
    q_latent = jnp.einsum(
        "rhk,chk->rhc", q_nope, key_block, preferred_element_type=jnp.float32
    ).astype(jnp.bfloat16)
    q_full = jnp.concatenate([q_latent, q_rope], axis=2)
    positions = jnp.repeat(
        span_ids, span_len, total_repeat_length=total_slots
    ) * span_len + jnp.tile(jnp.arange(span_len, dtype=jnp.int32), span_count)
    q_positions = lax.dynamic_slice_in_dim(positions, lax.axis_index("ctx") * row_count, row_count)
    queries = [
        q_full[slot_j * span_len : (slot_j + 1) * span_len].reshape(span_len * heads_dev, KV + ROPE)
        for slot_j in range(2)
    ]
    query_pos = [q_positions[slot_j * span_len : (slot_j + 1) * span_len] for slot_j in range(2)]

    def update(state, q_matrix, q_pos, key_rows, key_pos):
        highest, totals, running = state
        scores = (
            lax.dot_general(
                q_matrix, key_rows, (((1,), (1,)), ((), ())), preferred_element_type=jnp.float32
            )
            * softmax_scale
        )
        visible = key_pos[None, :] <= q_pos[:, None]
        visible = jnp.broadcast_to(
            visible[:, None, :], (q_pos.shape[0], heads_dev, key_pos.shape[0])
        ).reshape(q_matrix.shape[0], key_pos.shape[0])
        scores = jnp.where(visible, scores, -1e30)
        new_high = jnp.maximum(highest, jnp.max(scores, axis=1))
        weights = jnp.where(visible, jnp.exp(scores - new_high[:, None]), 0.0)
        totals = jnp.sum(weights, axis=1)
        running = jnp.dot(
            weights.astype(jnp.bfloat16), key_rows[:, :KV], preferred_element_type=jnp.float32
        )
        return (new_high, totals, running)

    def visit_span(state, slot_j, key_rows, key_pos):
        return lax.cond(
            jnp.min(key_pos) <= jnp.max(query_pos[slot_j]),
            lambda inner: update(inner, queries[slot_j], query_pos[slot_j], key_rows, key_pos),
            lambda inner: inner,
            state,
        )

    score_rows = span_len * heads_dev
    initial = tuple(
        (
            (
                jnp.full((score_rows,), -1e30, jnp.float32),
                jnp.zeros((score_rows,), jnp.float32),
                jnp.zeros((score_rows, KV), jnp.float32),
            )
            for slot_j in range(2)
        )
    )

    def fold_keys(states, shard_rows):
        key_pos = lax.slice_in_dim(positions, 0, shard_rows.shape[0], axis=0)
        return tuple(
            (visit_span(states[slot_j], slot_j, shard_rows, key_pos) for slot_j in range(2))
        )

    states = fold_keys(initial, lax.all_gather(latent, "ctx", axis=0, tiled=True))
    mixed = jnp.concatenate(
        [
            (states[slot_j][2] / states[slot_j][1][:, None])
            .astype(jnp.bfloat16)
            .reshape(span_len, heads_dev, KV)
            for slot_j in range(2)
        ],
        axis=0,
    )
    shard_rows = lax.all_gather(w_uv, "ctx", axis=0, tiled=True)
    value_block = shard_rows.reshape(shard_rows.shape[0], heads_dev, VDIM)
    result = jnp.einsum("rhc,chv->rhv", mixed, value_block, preferred_element_type=jnp.float32)
    return result.reshape(row_count, heads_dev * VDIM).astype(jnp.bfloat16)


def solution(mesh):
    placed = (P("ctx", "tp"), P("ctx", None), P(None, "tp"), P("ctx", "tp"), P("ctx", "tp"), P())
    return jax.shard_map(
        per_device, mesh=mesh, in_specs=placed, out_specs=P("ctx", "tp"), check_vma=False
    )
```

profile of v0, /device:TPU:1, one launch (start us, length us, event | category | flops | bytes accessed | tf_op | source)
XLA Modules:
  0.0 294.5 jit_solution(12755800408900300186)
XLA Ops:
  6.5 0.7 all-gather.4.cloned.1.call-update
  7.3 0.7 all-gather.8.cloned.1.call-update
  8.1 1.7 copy.31
  9.8 0.1 tile.14
  9.9 25.2 %all_gather.12 = bf16[128,1536]{0,1:T(8,128)(2,1)S(1)} all-gather(bf16[128,192]{0,1:T(8,128)(2,1)} %param.12), channel_id=1, replica_groups=mesh['ctx'=32,'tp'=8] {'tp'}, dimensions={1}, use_global_device_ids=true | all-gather | bytes 442368 | tf_op jit(solution)/shard_map/all_gather | solution.py:20
  35.1 3.2 %convolution_convert_fusion = bf16[128,1536]{1,0:T(8,128)(2,1)S(1)} fusion(bf16[128,1536]{0,1:T(8,128)(2,1)S(1)} %all_gather.12, bf16[1536,1536]{1,0:T(8,128)(2,1)} %param.14), kind=kOutput, calls=%fused_computation.38 | convolution fusion | flops 604176384 | bytes 5505024 | tf_op jit(solution)/shard_map/dot_general | solution.py:19
  38.3 0.2 copy.26
  38.5 0.2 copy.40
  38.7 0.1 broadcast.180
  38.8 0.1 reshape.182
  38.9 0.8 add_add_fusion.1
  39.7 0.1 add.86
  39.8 0.1 sub.31
  39.9 1.6 fusion.41
  41.5 2.1 fusion.38
  43.5 2.1 fusion.39
  45.6 2.1 fusion.40
  47.7 0.8 add_add_fusion.3
  48.5 4.5 %compare_select_fusion.1 = (s32[4096,1]{0,1:T(1,128)S(1)}, s32[4096,1]{0,1:T(1,128)S(1)}) fusion(s32[]{:T(128)} %bitcast.63, s32[]{:T(128)} %bitcast.64, s32[]{:T(128)} %bitcast.65, s32[]{:T(128)} %bitcast.66, s32[]{:T(128)} %bitcast.67, s32[]{:T(128)} %bitcast.69, s32[]{:T(128)} %bitcast.68, s32[4096,1]{0,1:T(1,128)S(1)} %bitcast.133, ...), kind=kLoop, calls=%fused_computation.109 | loop fusion | flops 57344 | bytes 65564 | tf_op jit(solution)/shard_map/jit(_take)/gather | solution.py:33
  53.0 2.9 compare_reduce_fusion.56
  55.9 35.8 %multiply_add_fusion = (s32[4096]{0:T(1024)S(1)}, s32[4096]{0:T(1024)S(1)}) fusion(s32[4096]{0:T(1024)S(1)} %tile.14, s32[32,128]{1,0:T(8,128)S(1)} %copy-done.1, s32[32]{0:T(128)S(1)} %iota_multiply_fusion, pred[4096]{0:T(1024)(128)(4,1)S(1)} %get-tuple-element.133, pred[4096]{0:T(1024)(128)(4,1)S(1)} %get-tuple-element.132, ...), kind=kLoop, calls=%fused_computation.122 | loop fusion | flops 278528 | bytes 315748 | tf_op jit(solution)/shard_map/add | solution.py:33
  91.7 0.1 dynamic_slice.3
  91.8 0.6 add_reduce_fusion
  92.4 0.7 slice_reduce_fusion.1
  95.7 1.5 copy.28
  97.2 72.0 %all-gather.8.cloned.1.call-done = bf16[512,1024]{1,0:T(8,128)(2,1)} async-done(((bf16[16,1024]{1,0:T(8,128)(2,1)}), bf16[512,1024]{1,0:T(8,128)(2,1)}) %all-gather.8.cloned.1.call-update) | async-done | bytes 1048592 | tf_op jit(solution)/shard_map/all_gather | solution.py:100
  169.2 2.3 copy.36
  171.5 0.5 fusion.30
  172.0 0.1 pad_maximum_fusion
  172.1 87.4 %all-gather.6.cloned.1.call-done = bf16[4096,576]{1,0:T(8,128)(2,1)} async-done(((bf16[128,576]{1,0:T(8,128)(2,1)}), bf16[4096,576]{1,0:T(8,128)(2,1)}) %all-gather.6.cloned.1.call-update) | async-done | bytes 4718608 | tf_op jit(solution)/shard_map/all_gather | solution.py:90
  259.5 13.2 %conditional.2 = (f32[512]{0:T(512)S(1)}, f32[512,512]{1,0:T(8,128)S(1)}) conditional(s32[]{:T(128)} %convert_element_type.36, () %tuple.25, (s32[4096]{0:T(1024)S(1)}, s32[64]{0:T(128)S(1)}, bf16[128,8,576]{2,0,1:T(8,128)(2,1)S(1)}, bf16[4096,576]{1,0:T(8,128)(2,1)}) %tuple.26), branch_computations={%region_2.3_spmd, %region_3.6_spmd} | conditional | flops 4590927360 | bytes 54948160 | solution.py:65
  259.5 0.2 broadcast_compare_fusion
  259.7 0.7 copy.32
  260.5 6.5 %fusion = (f32[512]{0:T(512)S(1)}, f32[512,4096]{1,0:T(8,128)S(1)}) fusion(pred[64,4096]{1,0:T(8,128)(4,1)S(1)} %broadcast_compare_fusion, bf16[4096,576]{1,0:T(8,128)(2,1)} %get-tuple-element.40, bf16[128,8,576]{2,1,0:T(8,128)(2,1)S(1)} %copy.32), kind=kOutput, calls=%fused_computation.2 | convolution fusion | flops 2422210048 | bytes 14026752 | tf_op jit(solution)/shard_map/cond/branch_1_fun/dot_general | solution.py:46
  267.1 2.6 fusion.3
  269.6 3.1 %fusion.2 = f32[512]{0:T(512)S(1)} fusion(f32[512,4096]{1,0:T(8,128)S(1)} %get-tuple-element.141, f32[512]{0:T(512)S(1)} %broadcast_maximum_fusion, pred[64,4096]{1,0:T(8,128)(4,1)S(1)} %broadcast_compare_fusion), kind=kLoop, calls=%fused_computation.4 | loop fusion | flops 10485248 | bytes 8654848 | tf_op jit(solution)/shard_map/cond/branch_1_fun/reduce_sum | solution.py:58
  272.7 0.1 fusion.34
  272.8 0.2 copy.34
  273.0 13.3 %conditional.3 = (f32[512]{0:T(512)S(1)}, f32[512,512]{1,0:T(8,128)S(1)}) conditional(s32[]{:T(128)} %convert_element_type.41, () %tuple.27, (s32[4096]{0:T(1024)S(1)}, s32[64]{0:T(128)S(1)}, bf16[128,8,576]{2,0,1:T(8,128)(2,1)S(1)}, bf16[4096,576]{1,0:T(8,128)(2,1)}) %tuple.28), branch_computations={%region_7.8_spmd, %region_8.11_spmd} | conditional | flops 4590927360 | bytes 54948160 | solution.py:65
  273.3 0.2 broadcast_compare_fusion.1
  273.5 0.7 copy.33
  274.2 6.5 %fusion.15 = (f32[512]{0:T(512)S(1)}, f32[512,4096]{1,0:T(8,128)S(1)}) fusion(pred[64,4096]{1,0:T(8,128)(4,1)S(1)} %broadcast_compare_fusion.1, bf16[4096,576]{1,0:T(8,128)(2,1)} %get-tuple-element.44, bf16[128,8,576]{2,1,0:T(8,128)(2,1)S(1)} %copy.33), kind=kOutput, calls=%fused_computation.21 | convolution fusion | flops 2422210048 | bytes 14026752 | tf_op jit(solution)/shard_map/cond/branch_1_fun/dot_general | solution.py:46
  280.8 2.5 fusion.18
  283.3 2.9 %fusion.17 = f32[512]{0:T(512)S(1)} fusion(f32[512,4096]{1,0:T(8,128)S(1)} %get-tuple-element.143, f32[512]{0:T(512)S(1)} %broadcast_maximum_fusion.1, pred[64,4096]{1,0:T(8,128)(4,1)S(1)} %broadcast_compare_fusion.1), kind=kLoop, calls=%fused_computation.23 | loop fusion | flops 10485248 | bytes 8654848 | tf_op jit(solution)/shard_map/cond/branch_1_fun/reduce_sum | solution.py:58
  286.3 0.1 fusion.35
  286.4 0.2 copy.35
  286.6 0.5 convolution_convert_fusion.2
  287.1 0.9 copy.37
  (24 shorter events, 0.2 us)
Async XLA Ops:
  6.5 49.4 %copy-start.1 = (s32[32,128]{1,0:T(8,128)S(1)}, s32[32,128]{1,0:T(8,128)}, u32[]{:S(2)}) copy-start(s32[32,128]{1,0:T(8,128)} %constant.125.clone.1) | copy-start | bytes 49156
  6.5 89.1 %all-gather.4.cloned.1.call-start = ((), (), s32[]{:S(2)}) async-start(), calls=%async_computation | async-start | bytes 1081344 | tf_op jit(solution)/shard_map/all_gather | solution.py:27
  7.3 161.9 %all-gather.8.cloned.1.call-start = ((), (), s32[]{:S(2)}) async-start(), calls=%async_computation.2 | async-start | bytes 1081344 | tf_op jit(solution)/shard_map/all_gather | solution.py:100
  8.0 251.5 %all-gather.6.cloned.1.call-start = ((), (), s32[]{:S(2)}) async-start(), calls=%async_computation.1 | async-start | bytes 5406720 | tf_op jit(solution)/shard_map/all_gather | solution.py:90
  259.7 7.3 %slice-start = ((s8[5242880]{0:T(1024)(128)(4,1)}), s8[4194304]{0:T(1024)(128)(4,1)S(1)}, s32[]{:S(2)}) async-start(s8[5242880]{0:T(1024)(128)(4,1)} %bitcast.135), calls=%async_computation.3 | async-start | bytes 8388608 | tf_op jit(solution)/shard_map/cond
  260.5 6.6 %slice-start.1 = ((s8[5242880]{0:T(1024)(128)(4,1)}), s8[1048576]{0:T(1024)(128)(4,1)S(1)}, s32[]{:S(2)}) async-start(s8[5242880]{0:T(1024)(128)(4,1)} %bitcast.135), calls=%async_computation.4 | async-start | bytes 2097152 | tf_op jit(solution)/shard_map/cond
  273.0 13.6 %copy-start = (bf16[512,1024]{0,1:T(8,128)(2,1)S(1)}, bf16[512,1024]{0,1:T(8,128)(2,1)}, u32[]{:S(2)}) copy-start(bf16[512,1024]{0,1:T(8,128)(2,1)} %copy.36) | copy-start | bytes 3145732
  273.5 7.3 %slice-start.2 = ((s8[5242880]{0:T(1024)(128)(4,1)}), s8[4194304]{0:T(1024)(128)(4,1)S(1)}, s32[]{:S(2)}) async-start(s8[5242880]{0:T(1024)(128)(4,1)} %bitcast.137), calls=%async_computation.5 | async-start | bytes 8388608 | tf_op jit(solution)/shard_map/cond
  274.2 6.6 %slice-start.3 = ((s8[5242880]{0:T(1024)(128)(4,1)}), s8[1048576]{0:T(1024)(128)(4,1)S(1)}, s32[]{:S(2)}) async-start(s8[5242880]{0:T(1024)(128)(4,1)} %bitcast.137), calls=%async_computation.6 | async-start | bytes 2097152 | tf_op jit(solution)/shard_map/cond
Sparse Core Ops, SparseCore 0:
  10.1 81.7 all-gather.3
  94.7 74.4 all-gather.7
  172.0 87.5 all-gather.5
where the time goes:
time: 295 us; the launch traced here: 294 us
  waiting for transfers between devices  161 us (55%)
  other arithmetic  53 us (18%)
  blocking collectives  25.2 us (9%)
  matrix products  22.2 us (8%)
  local copies, waits for them, and re-layouts  16.9 us (6%)
  between operations  15.7 us (5%)
    all_gather x1, waiting for transfers between devices, per_device(): lax.all_gather(latent, 'ctx', axis=0, tiled=True)  87.4 us
    all_gather x1, waiting for transfers between devices, per_device(): shard_rows = lax.all_gather(w_uv, 'ctx', axis=0, tiled=True)  72 us
    add x1, other arithmetic, per_device(): jnp.repeat(span_ids, span_len, total_repeat_length=total_slots) * span_len  35.8 us
    all_gather x1, blocking collectives, per_device(): lax.all_gather(compressed, 'tp', axis=1, tiled=True)  25.2 us
    dot_general x2, matrix products, update(): lax.dot_general(q_matrix, key_rows, (((1,), (1,)), ((), ())), preferred_e...  13.1 us
    gather x4, local copies, waits for them, and re-layouts, per_device(): jnp.repeat(span_ids, span_len, total_repeat_length=total_slots) * span_len  7.81 us
    gather x2, other arithmetic, per_device(): jnp.repeat(span_ids, span_len, total_repeat_length=total_slots) * span_len  7.4 us
    reduce_sum x2, other arithmetic, update(): totals = jnp.sum(weights, axis=1)  6.01 us
  transfers between devices with their start and end apart: 3, of which 2 were waited for; matrix products, arithmetic and copies ran while one was open for 22% of the time, Pallas kernels for 0%

commit v1 on v0

--- a/solution.py
+++ b/solution.py
@@ -1,3 +1,4 @@
+import functools
 import jax
 import jax.numpy as jnp
 from jax import lax
@@ -9,6 +10,18 @@
 KV = 512
 
 
+def page_link(matrix, chip_axis):
+    in_order = []
+    for _ in range(jax.lax.axis_size(chip_axis)):
+        in_order.append(matrix)
+    b_next = jnp.stack(in_order, 0)
+    reached = jax.lax.all_to_all(b_next, chip_axis, 0, 0)
+    return jnp.concatenate(reached, 1)
+
+
+_put_windows = functools.partial(page_link, chip_axis="tp")
+
+
 def per_device(compressed, latent, w_uq, w_uk, w_uv, span_ids):
     row_count = compressed.shape[0]
     span_len = row_count // 2
@@ -16,11 +29,7 @@
     span_count = span_ids.shape[0]
     total_slots = span_count * span_len
     softmax_scale = (NOPE + ROPE) ** (-0.5)
-    query_proj = jnp.dot(
-        lax.all_gather(compressed, "tp", axis=1, tiled=True),
-        w_uq,
-        preferred_element_type=jnp.float32,
-    )
+    query_proj = jnp.dot(_put_windows(compressed), w_uq, preferred_element_type=jnp.float32)
     query_proj = query_proj.astype(jnp.bfloat16).reshape(row_count, heads_dev, NOPE + ROPE)
     q_nope = query_proj[:, :, :NOPE]
     q_rope = query_proj[:, :, NOPE:]

time: 295 us -> 295 us (level)
  blocking collectives: 25.2 us -> 0 us
  waiting for transfers between devices: 161 us -> 178 us
  starting transfers between devices: 0.08 us -> 6.03 us
    all_gather x1 -> x0, blocking collectives: 25.2 us -> none  [per_device(): lax.all_gather(compressed, 'tp', axis=1, tiled=True)]
    all_gather x1, waiting for transfers between devices: 0.02 us -> 13.5 us  [per_device(): shard_rows = lax.all_gather(w_uk, 'ctx', axis=0, tiled=True)]
    all_to_all x0 -> x1, starting transfers between devices: none -> 5.95 us  [page_link(): reached = jax.lax.all_to_all(b_next, chip_axis, 0, 0)]
    all_gather x1, waiting for transfers between devices: 72 us -> 75.7 us  [per_device(): shard_rows = lax.all_gather(w_uv, 'ctx', axis=0, tiled=True)]
  transfers between devices with their start and end apart: 3 -> 4, of which waited for: 2 -> 3; matrix products, arithmetic and copies ran while one was open for 22% -> 23% of each run, Pallas kernels for 0% -> 0%
where the time goes in v1:
time: 295 us; the launch traced here: 294 us
  waiting for transfers between devices  178 us (60%)
  other arithmetic  53.4 us (18%)
  matrix products  22.2 us (8%)
  local copies, waits for them, and re-layouts  18.5 us (6%)
  between operations  15.8 us (5%)
  starting transfers between devices  6.03 us (2%)
    all_gather x1, waiting for transfers between devices, per_device(): lax.all_gather(latent, 'ctx', axis=0, tiled=True)  87.4 us
    all_gather x1, waiting for transfers between devices, per_device(): shard_rows = lax.all_gather(w_uv, 'ctx', axis=0, tiled=True)  75.7 us
    add x1, other arithmetic, per_device(): jnp.repeat(span_ids, span_len, total_repeat_length=total_slots) * span_len  36.3 us
    all_gather x1, waiting for transfers between devices, per_device(): shard_rows = lax.all_gather(w_uk, 'ctx', axis=0, tiled=True)  13.5 us
    dot_general x2, matrix products, update(): lax.dot_general(q_matrix, key_rows, (((1,), (1,)), ((), ())), preferred_e...  13.1 us
    gather x4, local copies, waits for them, and re-layouts, per_device(): jnp.repeat(span_ids, span_len, total_repeat_length=total_slots) * span_len  7.81 us
    gather x2, other arithmetic, per_device(): jnp.repeat(span_ids, span_len, total_repeat_length=total_slots) * span_len  7.38 us
    all_to_all x1, starting transfers between devices, page_link(): reached = jax.lax.all_to_all(b_next, chip_axis, 0, 0)  5.95 us
  transfers between devices with their start and end apart: 4, of which 3 were waited for; matrix products, arithmetic and copies ran while one was open for 23% of the time, Pallas kernels for 0%

profile of v1, /device:TPU:1, one launch (start us, length us, event | category | flops | bytes accessed | tf_op | source)
XLA Modules:
  0.0 294.3 jit_solution(8738837751825066108)
XLA Ops:
  6.5 0.7 all-gather.4.cloned.1.call-update
  7.3 0.7 all-gather.8.cloned.1.call-update
  8.1 1.7 copy.32
  9.8 1.6 stack.2
  11.4 5.9 %all-to-all-start = ((bf16[8,128,192]{1,2,0:T(8,128)(2,1)}), bf16[8,128,192]{1,2,0:T(8,128)(2,1)S(1)}, u32[]{:S(2)}, u32[]{:S(2)}) async-start(bf16[8,128,192]{1,2,0:T(8,128)(2,1)} %stack.2), calls=%async_computation | async-start | bytes 786432 | tf_op jit(solution)/shard_map/all_to_all | solution.py:18
  17.5 0.1 reshape.190
  17.6 1.6 fusion.41
  19.2 2.1 fusion.38
  21.3 2.1 fusion.39
  23.3 2.1 fusion.40
  25.4 0.8 add_add_fusion.3
  26.2 4.5 %compare_select_fusion.1 = (s32[4096,1]{0,1:T(1,128)S(1)}, s32[4096,1]{0,1:T(1,128)S(1)}) fusion(s32[]{:T(128)} %bitcast.63, s32[]{:T(128)} %bitcast.64, s32[]{:T(128)} %bitcast.65, s32[]{:T(128)} %bitcast.66, s32[]{:T(128)} %bitcast.67, s32[]{:T(128)} %bitcast.69, s32[]{:T(128)} %bitcast.68, s32[4096,1]{0,1:T(1,128)S(1)} %bitcast.137, ...), kind=kLoop, calls=%fused_computation.109 | loop fusion | flops 57344 | bytes 65564 | tf_op jit(solution)/shard_map/jit(_take)/gather | solution.py:42
  30.7 2.9 compare_reduce_fusion.56
  33.6 36.3 %multiply_add_fusion = (s32[4096]{0:T(1024)S(1)}, s32[4096]{0:T(1024)S(1)}) fusion(s32[4096]{0:T(1024)S(1)} %tile.14, s32[32,128]{1,0:T(8,128)} %constant.125.clone.1, s32[32]{0:T(128)S(1)} %iota_multiply_fusion, pred[4096]{0:T(1024)(128)(4,1)S(1)} %get-tuple-element.133, pred[4096]{0:T(1024)(128)(4,1)S(1)} %get-tuple-element.132, ...), kind=kLoop, calls=%fused_computation.122 | loop fusion | flops 278528 | bytes 315748 | tf_op jit(solution)/shard_map/add | solution.py:42
  69.9 0.8 add_add_fusion.1
  70.7 0.1 add.86
  70.8 0.1 sub.31
  70.8 0.1 dynamic_slice.3
  70.9 0.7 add_reduce_fusion
  71.6 0.7 slice_reduce_fusion.1
  74.9 3.2 %convolution_convert_fusion = bf16[128,1536]{1,0:T(8,128)(2,1)S(1)} fusion(bf16[128,1536]{0,1:T(8,128)(2,1)S(1)} %bitcast.133, bf16[1536,1536]{1,0:T(8,128)(2,1)} %param.14), kind=kOutput, calls=%fused_computation.38 | convolution fusion | flops 604176384 | bytes 5505024 | tf_op jit(solution)/shard_map/dot_general | solution.py:32
  78.0 0.2 copy.27
  78.3 0.2 copy.41
  78.5 13.5 %all-gather.4.cloned.1.call-done = bf16[512,1024]{1,0:T(8,128)(2,1)} async-done(((bf16[16,1024]{1,0:T(8,128)(2,1)}), bf16[512,1024]{1,0:T(8,128)(2,1)}) %all-gather.4.cloned.1.call-update) | async-done | bytes 1048592 | tf_op jit(solution)/shard_map/all_gather | solution.py:36
  91.9 1.5 copy.29
  93.4 75.7 %all-gather.8.cloned.1.call-done = bf16[512,1024]{1,0:T(8,128)(2,1)} async-done(((bf16[16,1024]{1,0:T(8,128)(2,1)}), bf16[512,1024]{1,0:T(8,128)(2,1)}) %all-gather.8.cloned.1.call-update) | async-done | bytes 1048592 | tf_op jit(solution)/shard_map/all_gather | solution.py:109
  169.2 2.3 copy.37
  171.5 0.5 fusion.30
  172.0 0.1 pad_maximum_fusion
  172.1 87.4 %all-gather.6.cloned.1.call-done = bf16[4096,576]{1,0:T(8,128)(2,1)} async-done(((bf16[128,576]{1,0:T(8,128)(2,1)}), bf16[4096,576]{1,0:T(8,128)(2,1)}) %all-gather.6.cloned.1.call-update) | async-done | bytes 4718608 | tf_op jit(solution)/shard_map/all_gather | solution.py:99
  259.5 13.0 %conditional.2 = (f32[512]{0:T(512)S(1)}, f32[512,512]{1,0:T(8,128)S(1)}) conditional(s32[]{:T(128)} %convert_element_type.36, () %tuple.25, (s32[4096]{0:T(1024)S(1)}, s32[64]{0:T(128)S(1)}, bf16[128,8,576]{2,0,1:T(8,128)(2,1)S(1)}, bf16[4096,576]{1,0:T(8,128)(2,1)}) %tuple.26), branch_computations={%region_2.3_spmd, %region_3.6_spmd} | conditional | flops 4590927360 | bytes 54948160 | solution.py:74
  259.5 0.2 broadcast_compare_fusion
  259.7 0.7 copy.33
  260.5 6.5 %fusion = (f32[512]{0:T(512)S(1)}, f32[512,4096]{1,0:T(8,128)S(1)}) fusion(pred[64,4096]{1,0:T(8,128)(4,1)S(1)} %broadcast_compare_fusion, bf16[4096,576]{1,0:T(8,128)(2,1)} %get-tuple-element.40, bf16[128,8,576]{2,1,0:T(8,128)(2,1)S(1)} %copy.33), kind=kOutput, calls=%fused_computation.2 | convolution fusion | flops 2422210048 | bytes 14026752 | tf_op jit(solution)/shard_map/cond/branch_1_fun/dot_general | solution.py:55
  267.1 2.5 fusion.3
  269.6 2.9 %fusion.2 = f32[512]{0:T(512)S(1)} fusion(f32[512,4096]{1,0:T(8,128)S(1)} %get-tuple-element.141, f32[512]{0:T(512)S(1)} %broadcast_maximum_fusion, pred[64,4096]{1,0:T(8,128)(4,1)S(1)} %broadcast_compare_fusion), kind=kLoop, calls=%fused_computation.4 | loop fusion | flops 10485248 | bytes 8654848 | tf_op jit(solution)/shard_map/cond/branch_1_fun/reduce_sum | solution.py:67
  272.5 0.1 fusion.34
  272.7 0.2 copy.35
  272.9 13.3 %conditional.3 = (f32[512]{0:T(512)S(1)}, f32[512,512]{1,0:T(8,128)S(1)}) conditional(s32[]{:T(128)} %convert_element_type.41, () %tuple.27, (s32[4096]{0:T(1024)S(1)}, s32[64]{0:T(128)S(1)}, bf16[128,8,576]{2,0,1:T(8,128)(2,1)S(1)}, bf16[4096,576]{1,0:T(8,128)(2,1)}) %tuple.28), branch_computations={%region_7.8_spmd, %region_8.11_spmd} | conditional | flops 4590927360 | bytes 54948160 | solution.py:74
  273.1 0.2 broadcast_compare_fusion.1
  273.3 0.7 copy.34
  274.1 6.5 %fusion.15 = (f32[512]{0:T(512)S(1)}, f32[512,4096]{1,0:T(8,128)S(1)}) fusion(pred[64,4096]{1,0:T(8,128)(4,1)S(1)} %broadcast_compare_fusion.1, bf16[4096,576]{1,0:T(8,128)(2,1)} %get-tuple-element.44, bf16[128,8,576]{2,1,0:T(8,128)(2,1)S(1)} %copy.34), kind=kOutput, calls=%fused_computation.21 | convolution fusion | flops 2422210048 | bytes 14026752 | tf_op jit(solution)/shard_map/cond/branch_1_fun/dot_general | solution.py:55
  280.7 2.5 fusion.18
  283.2 2.9 %fusion.17 = f32[512]{0:T(512)S(1)} fusion(f32[512,4096]{1,0:T(8,128)S(1)} %get-tuple-element.143, f32[512]{0:T(512)S(1)} %broadcast_maximum_fusion.1, pred[64,4096]{1,0:T(8,128)(4,1)S(1)} %broadcast_compare_fusion.1), kind=kLoop, calls=%fused_computation.23 | loop fusion | flops 10485248 | bytes 8654848 | tf_op jit(solution)/shard_map/cond/branch_1_fun/reduce_sum | solution.py:67
  286.1 0.1 fusion.35
  286.3 0.2 copy.36
  286.5 0.4 convolution_convert_fusion.2
  286.9 0.9 copy.38
  (24 shorter events, 0.3 us)
Async XLA Ops:
  6.5 85.4 %all-gather.4.cloned.1.call-start = ((), (), s32[]{:S(2)}) async-start(), calls=%async_computation.1 | async-start | bytes 1081344 | tf_op jit(solution)/shard_map/all_gather | solution.py:36
  7.3 161.9 %all-gather.8.cloned.1.call-start = ((), (), s32[]{:S(2)}) async-start(), calls=%async_computation.3 | async-start | bytes 1081344 | tf_op jit(solution)/shard_map/all_gather | solution.py:109
  8.0 251.5 %all-gather.6.cloned.1.call-start = ((), (), s32[]{:S(2)}) async-start(), calls=%async_computation.2 | async-start | bytes 5406720 | tf_op jit(solution)/shard_map/all_gather | solution.py:99
  11.4 63.5 %all-to-all-start = ((bf16[8,128,192]{1,2,0:T(8,128)(2,1)}), bf16[8,128,192]{1,2,0:T(8,128)(2,1)S(1)}, u32[]{:S(2)}, u32[]{:S(2)}) async-start(bf16[8,128,192]{1,2,0:T(8,128)(2,1)} %stack.2), calls=%async_computation | async-start | bytes 786432 | tf_op jit(solution)/shard_map/all_to_all | solution.py:18
  259.7 7.3 %slice-start = ((s8[5242880]{0:T(1024)(128)(4,1)}), s8[4194304]{0:T(1024)(128)(4,1)S(1)}, s32[]{:S(2)}) async-start(s8[5242880]{0:T(1024)(128)(4,1)} %bitcast.139), calls=%async_computation.4 | async-start | bytes 8388608 | tf_op jit(solution)/shard_map/cond
  260.5 6.6 %slice-start.1 = ((s8[5242880]{0:T(1024)(128)(4,1)}), s8[1048576]{0:T(1024)(128)(4,1)S(1)}, s32[]{:S(2)}) async-start(s8[5242880]{0:T(1024)(128)(4,1)} %bitcast.139), calls=%async_computation.5 | async-start | bytes 2097152 | tf_op jit(solution)/shard_map/cond
  272.9 13.6 %copy-start = (bf16[512,1024]{0,1:T(8,128)(2,1)S(1)}, bf16[512,1024]{0,1:T(8,128)(2,1)}, u32[]{:S(2)}) copy-start(bf16[512,1024]{0,1:T(8,128)(2,1)} %copy.37) | copy-start | bytes 3145732
  273.3 7.3 %slice-start.2 = ((s8[5242880]{0:T(1024)(128)(4,1)}), s8[4194304]{0:T(1024)(128)(4,1)S(1)}, s32[]{:S(2)}) async-start(s8[5242880]{0:T(1024)(128)(4,1)} %bitcast.141), calls=%async_computation.6 | async-start | bytes 8388608 | tf_op jit(solution)/shard_map/cond
  274.1 6.6 %slice-start.3 = ((s8[5242880]{0:T(1024)(128)(4,1)}), s8[1048576]{0:T(1024)(128)(4,1)S(1)}, s32[]{:S(2)}) async-start(s8[5242880]{0:T(1024)(128)(4,1)} %bitcast.141), calls=%async_computation.7 | async-start | bytes 2097152 | tf_op jit(solution)/shard_map/cond
Sparse Core Ops, SparseCore 0:
  10.1 81.7 all-gather.3
  94.7 74.4 all-gather.7
  171.9 87.5 all-gather.5
